TPU v7x, 128 devices: a whole 4x4x4 slice. The times are simulated.
128 devices in a mesh: smp: 8 (over y, core), gx: 8 (over z_lo, x), gz: 2 (over z_hi).
Axes of the slice: x: 4, y: 4, z: 4 (z_hi: 2, z_lo: 2; z = z_hi * 2 + z_lo), core: 2. Of those that a mesh axis runs over, the one named last changes fastest.
Arguments:
- features: bfloat16 [8, 32, 40, 8, 256], P('smp', None, 'gx', None, 'gz'), may hold values from -6 to 6
- first_weight: bfloat16 [32, 3, 3, 3, 32], replicated, may hold values from -0.21875 to 0.21875
- first_bias: float32 [32], replicated, may hold values from -1 to 1
- second_weight: bfloat16 [32, 3, 3, 3, 32], replicated, may hold values from -0.21875 to 0.21875
- second_bias: float32 [32], replicated, may hold values from -1 to 1
- cotangent: bfloat16 [8, 32, 40, 8, 256], P('smp', None, 'gx', None, 'gz'), may hold values from -6 to 6
Outputs:
- output: bfloat16 [8, 32, 40, 8, 256], P('smp', None, 'gx', None, 'gz')
- first_grad: float32 [32, 3, 3, 3, 32], replicated
- first_bias_grad: float32 [32], replicated
- second_grad: float32 [32, 3, 3, 3, 32], replicated
- second_bias_grad: float32 [32], replicated
All inputs are finite; a program needn't handle non-finite values.
Results may differ from a plain program's by a relative error of at most 0.011.
Values may be sent and summed in bfloat16 or wider, within the bound.
A program may use at most 128 MiB of HBM per device.

v0:
```python
import jax
import jax.numpy as jnp
from jax import lax
from jax.sharding import PartitionSpec as P


def extended(array, sides, width):
    for axis, dim in sides:
        size, length = (lax.axis_size(axis), array.shape[dim])
        up = [(i, (i + 1) % size) for i in range(size)]
        down = [(j, i) for i, j in up]
        last = lax.slice_in_dim(array, length - width, length, axis=dim)
        initial = lax.slice_in_dim(array, 0, width, axis=dim)
        before = lax.ppermute(last, axis, up)
        after = lax.ppermute(initial, axis, down)
        array = jnp.concatenate([before, array, after], axis=dim)
    return array


def wall_pad(field_in):
    return jnp.pad(field_in, ((0, 0), (0, 0), (0, 0), (1, 1), (0, 0)))


def extend(field_in, depth_cells):
    both_wide = extended(field_in, (("gx", 2), ("gz", 4)), depth_cells)
    return wall_pad(both_wide)


def stack_taps(padded, offset_x, offset_y, cells_x, cells_y, cells_z):
    return jnp.concatenate(
        [
            padded[
                :,
                :,
                offset_x : offset_x + cells_x,
                offset_y : offset_y + cells_y,
                offset_z : offset_z + cells_z,
            ]
            for offset_z in range(3)
        ],
        axis=1,
    )


def convolve(padded, weight):
    cells_x = padded.shape[2] - 2
    cells_y = padded.shape[3] - 2
    cells_z = padded.shape[4] - 2
    summed = jnp.zeros((padded.shape[0], weight.shape[0], cells_x, cells_y, cells_z), jnp.float32)
    for offset_x in range(3):
        for offset_y in range(3):
            stacked = stack_taps(padded, offset_x, offset_y, cells_x, cells_y, cells_z)
            tap_block = weight[:, offset_x, offset_y].reshape(weight.shape[0], -1)
            summed = summed + jnp.einsum(
                "ok,skxyz->soxyz", tap_block, stacked, preferred_element_type=jnp.float32
            )
    return summed


def correlate(upstream, padded):
    cells_x = upstream.shape[2]
    cells_y = upstream.shape[3]
    cells_z = upstream.shape[4]
    outer_terms = []
    for offset_x in range(3):
        inner_terms = []
        for offset_y in range(3):
            stacked = stack_taps(padded, offset_x, offset_y, cells_x, cells_y, cells_z)
            local_term = jnp.einsum(
                "soxyz,skxyz->ok", upstream, stacked, preferred_element_type=jnp.float32
            )
            inner_terms.append(local_term.reshape(upstream.shape[1], 3, -1))
        outer_terms.append(jnp.stack(inner_terms, axis=1))
    return jnp.stack(outer_terms, axis=1)


def shards(features, first_weight, first_bias, second_weight, second_bias, cotangent):
    input_pad = extend(features, 1)
    preact = convolve(input_pad, first_weight) + first_bias[None, :, None, None, None]
    hidden = jax.nn.silu(preact).astype(jnp.bfloat16)
    hidden_pad = extend(hidden, 1)
    residual_term = convolve(hidden_pad, second_weight) + second_bias[None, :, None, None, None]
    output = (features.astype(jnp.float32) + residual_term).astype(jnp.bfloat16)
    cells_all = (
        features.shape[0]
        * lax.axis_size("smp")
        * features.shape[2]
        * lax.axis_size("gx")
        * features.shape[3]
        * features.shape[4]
        * lax.axis_size("gz")
    )
    grad_scale = 1.0 / cells_all**0.5
    second_grad = correlate(cotangent, hidden_pad) * grad_scale
    second_bgrad = jnp.sum(cotangent, axis=(0, 2, 3, 4), dtype=jnp.float32) * grad_scale
    flipped = jnp.transpose(jnp.flip(second_weight, (1, 2, 3)), (4, 1, 2, 3, 0))
    upstream_pad = extend(cotangent, 1)
    hidden_grad = convolve(upstream_pad, flipped)
    logistic = jax.nn.sigmoid(preact)
    preact_grad = (hidden_grad * logistic * (1.0 + preact * (1.0 - logistic))).astype(jnp.bfloat16)
    first_grad = correlate(preact_grad, input_pad) * grad_scale
    first_bgrad = jnp.sum(preact_grad, axis=(0, 2, 3, 4), dtype=jnp.float32) * grad_scale
    first_grad, first_bgrad, second_grad, second_bgrad = lax.psum(
        (first_grad, first_bgrad, second_grad, second_bgrad), ("smp", "gx", "gz")
    )
    return (output, first_grad, first_bgrad, second_grad, second_bgrad)


def solution(mesh):
    in_specs = (
        P("smp", None, "gx", None, "gz"),
        P(),
        P(),
        P(),
        P(),
        P("smp", None, "gx", None, "gz"),
    )
    out_specs = (P("smp", None, "gx", None, "gz"), P(), P(), P(), P())
    return jax.shard_map(shards, mesh=mesh, in_specs=in_specs, out_specs=out_specs, check_vma=False)
```

profile of v0, /device:TPU:1, one launch (start us, length us, event | category | flops | bytes accessed | tf_op | source)
XLA Modules:
  0.0 336.7 jit_solution(1771370892015134245)
XLA Ops:
  7.2 1.1 copy.113
  8.3 4.7 %collective-permute-start.9 = (bf16[1,32,1,8,128]{4,1,3,2,0:T(8,128)(2,1)S(1)}, bf16[1,32,1,8,128]{4,1,3,2,0:T(8,128)(2,1)S(1)}, u32[]{:S(2)}, u32[]{:S(2)}) collective-permute-start(bf16[1,32,1,8,128]{4,1,3,2,0:T(8,128)(2,1)S(1)} %get-tuple-element.105), channel_id=1, source_target_pairs={{2,0},{4,2},{6,4},{8,6},{10,8},{12,10},{14,12},{0,14},{3,1},{5,3},... | collective-permute-start | bytes 196616 | tf_op jit(solution)/shard_map/ppermute | solution.py:15
  13.1 1.1 copy.88
  14.2 3.6 %collective-permute-start.1 = (bf16[1,32,1,8,128]{4,1,3,2,0:T(8,128)(2,1)S(1)}, bf16[1,32,1,8,128]{4,1,3,2,0:T(8,128)(2,1)S(1)}, u32[]{:S(2)}, u32[]{:S(2)}) collective-permute-start(bf16[1,32,1,8,128]{4,1,3,2,0:T(8,128)(2,1)S(1)} %get-tuple-element.109), channel_id=1, source_target_pairs={{2,0},{4,2},{6,4},{8,6},{10,8},{12,10},{14,12},{0,14},{3,1},{5,3},... | collective-permute-start | bytes 196616 | tf_op jit(solution)/shard_map/ppermute | solution.py:15
  20.6 2.4 collective-permute-done
  23.1 3.4 %collective-permute-start.10 = (bf16[1,32,7,8,1]{4,1,3,2,0:T(8,128)(2,1)S(1)}, bf16[1,32,7,8,1]{4,1,3,2,0:T(8,128)(2,1)S(1)}, u32[]{:S(2)}, u32[]{:S(2)}) collective-permute-start(bf16[1,32,7,8,1]{4,1,3,2,0:T(8,128)(2,1)S(1)} %get-tuple-element.89), channel_id=1, source_target_pairs={{0,1},{1,0},{2,3},{3,2},{4,5},{5,4},{6,7},{7,6},{8,9},{9,8},{10,11... | collective-permute-start | bytes 10760 | tf_op jit(solution)/shard_map/ppermute | solution.py:14
  26.8 3.0 collective-permute-start.2
  29.8 4.7 %collective-permute-done.10 = bf16[1,32,7,8,1]{4,1,3,2,0:T(8,128)(2,1)S(1)} collective-permute-done((bf16[1,32,7,8,1]{4,1,3,2,0:T(8,128)(2,1)S(1)}, bf16[1,32,7,8,1]{4,1,3,2,0:T(8,128)(2,1)S(1)}, u32[]{:S(2)}, u32[]{:S(2)}) %collective-permute-start.10) | collective-permute-done | bytes 3616 | tf_op jit(solution)/shard_map/ppermute | solution.py:14
  34.5 9.8 %collective-permute-done.11 = bf16[1,32,7,8,1]{4,1,3,2,0:T(8,128)(2,1)S(1)} collective-permute-done((bf16[1,32,7,8,1]{4,1,3,2,0:T(8,128)(2,1)S(1)}, bf16[1,32,7,8,1]{4,1,3,2,0:T(8,128)(2,1)S(1)}, u32[]{:S(2)}, u32[]{:S(2)}) %collective-permute-start.11) | collective-permute-done | bytes 3616 | tf_op jit(solution)/shard_map/ppermute | solution.py:15
  44.9 1.5 fusion.148
  46.5 7.7 %collective-permute-done.2 = bf16[1,32,7,8,1]{4,1,3,2,0:T(8,128)(2,1)S(1)} collective-permute-done((bf16[1,32,7,8,1]{4,1,3,2,0:T(8,128)(2,1)S(1)}, bf16[1,32,7,8,1]{4,1,3,2,0:T(8,128)(2,1)S(1)}, u32[]{:S(2)}, u32[]{:S(2)}) %collective-permute-start.2) | collective-permute-done | bytes 3616 | tf_op jit(solution)/shard_map/ppermute | solution.py:14
  54.2 9.8 %collective-permute-done.3 = bf16[1,32,7,8,1]{4,1,3,2,0:T(8,128)(2,1)S(1)} collective-permute-done((bf16[1,32,7,8,1]{4,1,3,2,0:T(8,128)(2,1)S(1)}, bf16[1,32,7,8,1]{4,1,3,2,0:T(8,128)(2,1)S(1)}, u32[]{:S(2)}, u32[]{:S(2)}) %collective-permute-start.3) | collective-permute-done | bytes 3616 | tf_op jit(solution)/shard_map/ppermute | solution.py:15
  64.6 1.5 fusion.150
  67.1 1.1 pad_maximum_fusion.14
  74.2 1.0 convolution_add_fusion.1
  76.6 0.7 convolution_bitcast_fusion.5
  78.7 0.7 convolution_bitcast_fusion.1
  79.4 0.7 convolution_bitcast_fusion.7
  81.6 0.7 convolution_bitcast_fusion
  82.4 3.6 %collective-permute-start.5 = (bf16[1,32,1,8,128]{4,1,3,2,0:T(8,128)(2,1)S(1)}, bf16[1,32,1,8,128]{4,1,3,2,0:T(8,128)(2,1)S(1)}, u32[]{:S(2)}, u32[]{:S(2)}) collective-permute-start(bf16[1,32,1,8,128]{4,1,3,2,0:T(8,128)(2,1)S(1)} %get-tuple-element.108), channel_id=1, source_target_pairs={{2,0},{4,2},{6,4},{8,6},{10,8},{12,10},{14,12},{0,14},{3,1},{5,3},... | collective-permute-start | bytes 196616 | tf_op jit(solution)/shard_map/ppermute | solution.py:15
  86.0 1.6 collective-permute-done.4
  87.9 2.8 collective-permute-start.6
  91.0 0.8 maximum_multiply_fusion
  91.8 78.4 %all-reduce.3 = (f32[32]{0:T(128)}, f32[32]{0:T(128)}) all-reduce(f32[32]{0:T(128)S(1)} %broadcast_multiply_fusion.1, f32[32]{0:T(128)S(1)} %broadcast_multiply_fusion), channel_id=1, replica_groups=mesh['smp'=8,'gx'=8,'gz'=2] {'smp','gx','gz'}, use_global_device_ids=true, to_apply=%region_2.3 | all-reduce | flops 64 | bytes 512 | tf_op jit(solution)/shard_map/psum | solution.py:103
  174.4 1.4 fusion.149
  176.7 0.7 convolution_bitcast_fusion.9
  180.3 0.7 convolution_bitcast_fusion.15
  183.0 0.8 maximum_multiply_fusion.1
  184.1 0.9 copy.164
  185.0 142.2 %all-reduce.7.cloned.1.call-done = (f32[32,3,3,3,32]{4,0,3,2,1:T(8,128)}, f32[32,3,3,3,32]{4,0,3,2,1:T(8,128)}) async-done(((f32[32,3,3,3,32]{4,0,3,2,1:T(8,128)}, f32[32,3,3,3,32]{4,0,3,2,1:T(8,128)}), (f32[32,3,3,3,32]{4,0,3,2,1:T(8,128)}, f32[32,3,3,3,32]{4,0,3,2,1:T(8,128)})) %all-reduce.7.cloned.1.call-update) | async-done | bytes 221200 | tf_op jit(solution)/shard_map/psum | solution.py:103
  327.2 1.9 copy.328
  329.1 0.8 copy.329
  (142 shorter events, 26.3 us)
Async XLA Ops:
  7.2 10.6 %copy-start = (bf16[1,32,5,8,128]{4,3,2,1,0:T(8,128)(2,1)S(1)}, bf16[1,32,5,8,128]{4,3,2,1,0:T(8,128)(2,1)}, u32[]{:S(2)}) copy-start(bf16[1,32,5,8,128]{4,3,2,1,0:T(8,128)(2,1)} %param.11) | copy-start | bytes 983044
  7.2 10.9 %copy-start.2 = (bf16[32,3,3,3,32]{4,0,3,2,1:T(8,128)(2,1)S(1)}, bf16[32,3,3,3,32]{4,0,3,2,1:T(8,128)(2,1)}, u32[]{:S(2)}) copy-start(bf16[32,3,3,3,32]{4,0,3,2,1:T(8,128)(2,1)} %param.9) | copy-start | bytes 165892
  7.2 320.0 %all-reduce.7.cloned.1.call-start = ((), (), s32[]{:S(2)}) async-start(), calls=%async_computation | async-start | bytes 1769472 | tf_op jit(solution)/shard_map/psum | solution.py:103
  8.3 12.0 %collective-permute-start.9 = (bf16[1,32,1,8,128]{4,1,3,2,0:T(8,128)(2,1)S(1)}, bf16[1,32,1,8,128]{4,1,3,2,0:T(8,128)(2,1)S(1)}, u32[]{:S(2)}, u32[]{:S(2)}) collective-permute-start(bf16[1,32,1,8,128]{4,1,3,2,0:T(8,128)(2,1)S(1)} %get-tuple-element.105), channel_id=1, source_target_pairs={{2,0},{4,2},{6,4},{8,6},{10,8},{12,10},{14,12},{0,14},{3,1},{5,3},... | collective-permute-start | bytes 196616 | tf_op jit(solution)/shard_map/ppermute | solution.py:15
  13.1 5.1 %copy-start.4 = (bf16[32,3,3,3,32]{4,0,3,2,1:T(8,128)(2,1)S(1)}, bf16[32,3,3,3,32]{4,0,3,2,1:T(8,128)(2,1)}, u32[]{:S(2)}) copy-start(bf16[32,3,3,3,32]{4,0,3,2,1:T(8,128)(2,1)} %param.7) | copy-start | bytes 165892
  13.1 7.2 %collective-permute-start.8 = (bf16[1,32,1,8,128]{4,1,3,2,0:T(8,128)(2,1)S(1)}, bf16[1,32,1,8,128]{4,1,3,2,0:T(8,128)(2,1)S(1)}, u32[]{:S(2)}, u32[]{:S(2)}) collective-permute-start(bf16[1,32,1,8,128]{4,1,3,2,0:T(8,128)(2,1)S(1)} %get-tuple-element.106), channel_id=1, source_target_pairs={{0,2},{2,4},{4,6},{6,8},{8,10},{10,12},{12,14},{14,0},{1,3},{3,5},... | collective-permute-start | bytes 196616 | tf_op jit(solution)/shard_map/ppermute | solution.py:14
  14.2 12.4 %collective-permute-start.1 = (bf16[1,32,1,8,128]{4,1,3,2,0:T(8,128)(2,1)S(1)}, bf16[1,32,1,8,128]{4,1,3,2,0:T(8,128)(2,1)S(1)}, u32[]{:S(2)}, u32[]{:S(2)}) collective-permute-start(bf16[1,32,1,8,128]{4,1,3,2,0:T(8,128)(2,1)S(1)} %get-tuple-element.109), channel_id=1, source_target_pairs={{2,0},{4,2},{6,4},{8,6},{10,8},{12,10},{14,12},{0,14},{3,1},{5,3},... | collective-permute-start | bytes 196616 | tf_op jit(solution)/shard_map/ppermute | solution.py:15
  17.8 5.2 %collective-permute-start = (bf16[1,32,1,8,128]{4,1,3,2,0:T(8,128)(2,1)S(1)}, bf16[1,32,1,8,128]{4,1,3,2,0:T(8,128)(2,1)S(1)}, u32[]{:S(2)}, u32[]{:S(2)}) collective-permute-start(bf16[1,32,1,8,128]{4,1,3,2,0:T(8,128)(2,1)S(1)} %get-tuple-element.110), channel_id=1, source_target_pairs={{0,2},{2,4},{4,6},{6,8},{8,10},{10,12},{12,14},{14,0},{1,3},{3,5},... | collective-permute-start | bytes 196616 | tf_op jit(solution)/shard_map/ppermute | solution.py:14
  20.3 2.7 copy-start.1
  23.1 11.4 %collective-permute-start.10 = (bf16[1,32,7,8,1]{4,1,3,2,0:T(8,128)(2,1)S(1)}, bf16[1,32,7,8,1]{4,1,3,2,0:T(8,128)(2,1)S(1)}, u32[]{:S(2)}, u32[]{:S(2)}) collective-permute-start(bf16[1,32,7,8,1]{4,1,3,2,0:T(8,128)(2,1)S(1)} %get-tuple-element.89), channel_id=1, source_target_pairs={{0,1},{1,0},{2,3},{3,2},{4,5},{5,4},{6,7},{7,6},{8,9},{9,8},{10,11... | collective-permute-start | bytes 10760 | tf_op jit(solution)/shard_map/ppermute | solution.py:14
  26.5 17.9 %collective-permute-start.11 = (bf16[1,32,7,8,1]{4,1,3,2,0:T(8,128)(2,1)S(1)}, bf16[1,32,7,8,1]{4,1,3,2,0:T(8,128)(2,1)S(1)}, u32[]{:S(2)}, u32[]{:S(2)}) collective-permute-start(bf16[1,32,7,8,1]{4,1,3,2,0:T(8,128)(2,1)S(1)} %get-tuple-element.90), channel_id=1, source_target_pairs={{1,0},{0,1},{3,2},{2,3},{5,4},{4,5},{7,6},{6,7},{9,8},{8,9},{11,10... | collective-permute-start | bytes 10760 | tf_op jit(solution)/shard_map/ppermute | solution.py:15
  26.8 27.4 %collective-permute-start.2 = (bf16[1,32,7,8,1]{4,1,3,2,0:T(8,128)(2,1)S(1)}, bf16[1,32,7,8,1]{4,1,3,2,0:T(8,128)(2,1)S(1)}, u32[]{:S(2)}, u32[]{:S(2)}) collective-permute-start(bf16[1,32,7,8,1]{4,1,3,2,0:T(8,128)(2,1)S(1)} %get-tuple-element.97), channel_id=1, source_target_pairs={{0,1},{1,0},{2,3},{3,2},{4,5},{5,4},{6,7},{7,6},{8,9},{9,8},{10,11... | collective-permute-start | bytes 10760 | tf_op jit(solution)/shard_map/ppermute | solution.py:14
  29.8 34.3 %collective-permute-start.3 = (bf16[1,32,7,8,1]{4,1,3,2,0:T(8,128)(2,1)S(1)}, bf16[1,32,7,8,1]{4,1,3,2,0:T(8,128)(2,1)S(1)}, u32[]{:S(2)}, u32[]{:S(2)}) collective-permute-start(bf16[1,32,7,8,1]{4,1,3,2,0:T(8,128)(2,1)S(1)} %get-tuple-element.98), channel_id=1, source_target_pairs={{1,0},{0,1},{3,2},{2,3},{5,4},{4,5},{7,6},{6,7},{9,8},{8,9},{11,10... | collective-permute-start | bytes 10760 | tf_op jit(solution)/shard_map/ppermute | solution.py:15
  70.4 0.7 copy-start.5
  82.3 5.3 %collective-permute-start.4 = (bf16[1,32,1,8,128]{4,1,3,2,0:T(8,128)(2,1)S(1)}, bf16[1,32,1,8,128]{4,1,3,2,0:T(8,128)(2,1)S(1)}, u32[]{:S(2)}, u32[]{:S(2)}) collective-permute-start(bf16[1,32,1,8,128]{4,1,3,2,0:T(8,128)(2,1)S(1)} %get-tuple-element.107), channel_id=1, source_target_pairs={{0,2},{2,4},{4,6},{6,8},{8,10},{10,12},{12,14},{14,0},{1,3},{3,5},... | collective-permute-start | bytes 196616 | tf_op jit(solution)/shard_map/ppermute | solution.py:14
  82.4 5.2 %collective-permute-start.5 = (bf16[1,32,1,8,128]{4,1,3,2,0:T(8,128)(2,1)S(1)}, bf16[1,32,1,8,128]{4,1,3,2,0:T(8,128)(2,1)S(1)}, u32[]{:S(2)}, u32[]{:S(2)}) collective-permute-start(bf16[1,32,1,8,128]{4,1,3,2,0:T(8,128)(2,1)S(1)} %get-tuple-element.108), channel_id=1, source_target_pairs={{2,0},{4,2},{6,4},{8,6},{10,8},{12,10},{14,12},{0,14},{3,1},{5,3},... | collective-permute-start | bytes 196616 | tf_op jit(solution)/shard_map/ppermute | solution.py:15
  87.9 82.2 %collective-permute-start.6 = (bf16[1,32,7,8,1]{4,1,3,2,0:T(8,128)(2,1)S(1)}, bf16[1,32,7,8,1]{4,1,3,2,0:T(8,128)(2,1)S(1)}, u32[]{:S(2)}, u32[]{:S(2)}) collective-permute-start(bf16[1,32,7,8,1]{4,1,3,2,0:T(8,128)(2,1)S(1)} %get-tuple-element.93), channel_id=1, source_target_pairs={{0,1},{1,0},{2,3},{3,2},{4,5},{5,4},{6,7},{7,6},{8,9},{9,8},{10,11... | collective-permute-start | bytes 10760 | tf_op jit(solution)/shard_map/ppermute | solution.py:14
  90.7 79.5 %collective-permute-start.7 = (bf16[1,32,7,8,1]{4,1,3,2,0:T(8,128)(2,1)S(1)}, bf16[1,32,7,8,1]{4,1,3,2,0:T(8,128)(2,1)S(1)}, u32[]{:S(2)}, u32[]{:S(2)}) collective-permute-start(bf16[1,32,7,8,1]{4,1,3,2,0:T(8,128)(2,1)S(1)} %get-tuple-element.94), channel_id=1, source_target_pairs={{1,0},{0,1},{3,2},{2,3},{5,4},{4,5},{7,6},{6,7},{9,8},{8,9},{11,10... | collective-permute-start | bytes 10760 | tf_op jit(solution)/shard_map/ppermute | solution.py:15
  182.9 0.9 copy-start.6
  327.2 1.9 copy-start.3
Sparse Core Ops, SparseCore 0:
  184.0 143.2 all-reduce.6
where the time goes:
time: 337 us
  waiting for transfers between devices  178 us (53%)
  blocking collectives  78.4 us (23%)
  starting transfers between devices  21.6 us (6%)
  matrix products  21.5 us (6%)
  between operations  14.6 us (4%)
  local copies, waits for them, and re-layouts  14 us (4%)
  other arithmetic  8.32 us (2%)
    psum x1, waiting for transfers between devices, shards(): lax.psum((first_grad, first_bgrad, second_grad, second_bgrad), ('smp', 'g...  142 us
    psum x1, blocking collectives, shards(): lax.psum((first_grad, first_bgrad, second_grad, second_bgrad), ('smp', 'g...  78.4 us
    ppermute x6, waiting for transfers between devices, extended(): after = lax.ppermute(initial, axis, down)  19.7 us
    ppermute x6, waiting for transfers between devices, extended(): before = lax.ppermute(last, axis, up)  16.3 us
    dot_general x18, matrix products, correlate(): jnp.einsum('soxyz,skxyz->ok', upstream, stacked, preferred_element_type=j...  12.8 us
    ppermute x6, starting transfers between devices, extended(): after = lax.ppermute(initial, axis, down)  12.4 us
    ppermute x6, starting transfers between devices, extended(): before = lax.ppermute(last, axis, up)  9.18 us
    dot_general x27, matrix products, convolve(): jnp.einsum('ok,skxyz->soxyz', tap_block, stacked, preferred_element_type=...  8.76 us
  transfers between devices with their start and end apart: 13, of which 7 were waited for; matrix products, arithmetic and copies ran while one was open for 2% of the time, Pallas kernels for 0%

commit v1 on v0

--- a/solution.py
+++ b/solution.py
@@ -101,7 +101,7 @@
     first_grad = correlate(preact_grad, input_pad) * grad_scale
     first_bgrad = jnp.sum(preact_grad, axis=(0, 2, 3, 4), dtype=jnp.float32) * grad_scale
     first_grad, first_bgrad, second_grad, second_bgrad = lax.psum(
-        (first_grad, first_bgrad, second_grad, second_bgrad), ("smp", "gx", "gz")
+        lax.psum((first_grad, first_bgrad, second_grad, second_bgrad), "smp"), ("gx", "gz")
     )
     return (output, first_grad, first_bgrad, second_grad, second_bgrad)
 

time: 337 us -> 319 us (0.947)
  blocking collectives: 78.4 us -> 52.4 us
  waiting for transfers between devices: 178 us -> 182 us
  matrix products: 21.5 us -> 25.4 us
    psum x1 -> x2, blocking collectives: 78.4 us -> 52.4 us  [the longest x1 35 us: shards(): lax.psum(lax.psum((first_grad, first_bgrad, second_grad, second_bgrad), '...]
    dot_general x27, matrix products: 8.76 us -> 12.6 us  [convolve(): jnp.einsum('ok,skxyz->soxyz', tap_block, stacked, preferred_element_type=...]
    psum x1 -> x2, waiting for transfers between devices: 142 us -> 146 us  [the longest x1 87.8 us: shards(): lax.psum(lax.psum((first_grad, first_bgrad, second_grad, second_bgrad), '...]
  transfers between devices with their start and end apart: 13 -> 14, of which waited for: 7 -> 8; matrix products, arithmetic and copies ran while one was open for 2% -> 4% of each run, Pallas kernels for 0% -> 0%
where the time goes in v1:
time: 319 us; the launch traced here: 318 us
  waiting for transfers between devices  182 us (57%)
  blocking collectives  52.4 us (16%)
  matrix products  25.4 us (8%)
  starting transfers between devices  21.6 us (7%)
  between operations  14.6 us (5%)
  local copies, waits for them, and re-layouts  14 us (4%)
  other arithmetic  8.32 us (3%)
    psum x1, waiting for transfers between devices, shards(): lax.psum(lax.psum((first_grad, first_bgrad, second_grad, second_bgrad), '...  87.8 us
    psum x1, waiting for transfers between devices, shards(): lax.psum((first_grad, first_bgrad, second_grad, second_bgrad), 'smp')  58.4 us
    psum x1, blocking collectives, shards(): lax.psum(lax.psum((first_grad, first_bgrad, second_grad, second_bgrad), '...  35 us
    ppermute x6, waiting for transfers between devices, extended(): after = lax.ppermute(initial, axis, down)  19.7 us
    psum x1, blocking collectives, shards(): lax.psum((first_grad, first_bgrad, second_grad, second_bgrad), 'smp')  17.4 us
    ppermute x6, waiting for transfers between devices, extended(): before = lax.ppermute(last, axis, up)  16.3 us
    dot_general x18, matrix products, correlate(): jnp.einsum('soxyz,skxyz->ok', upstream, stacked, preferred_element_type=j...  12.7 us
    dot_general x27, matrix products, convolve(): jnp.einsum('ok,skxyz->soxyz', tap_block, stacked, preferred_element_type=...  12.6 us
  transfers between devices with their start and end apart: 14, of which 8 were waited for; matrix products, arithmetic and copies ran while one was open for 4% of the time, Pallas kernels for 0%

profile of v1, /device:TPU:1, one launch (start us, length us, event | category | flops | bytes accessed | tf_op | source)
XLA Modules:
  0.0 318.5 jit_solution(8686939973801871798)
XLA Ops:
  7.2 1.1 copy.113
  8.3 4.7 %collective-permute-start.9 = (bf16[1,32,1,8,128]{4,1,3,2,0:T(8,128)(2,1)S(1)}, bf16[1,32,1,8,128]{4,1,3,2,0:T(8,128)(2,1)S(1)}, u32[]{:S(2)}, u32[]{:S(2)}) collective-permute-start(bf16[1,32,1,8,128]{4,1,3,2,0:T(8,128)(2,1)S(1)} %get-tuple-element.109), channel_id=1, source_target_pairs={{2,0},{4,2},{6,4},{8,6},{10,8},{12,10},{14,12},{0,14},{3,1},{5,3},... | collective-permute-start | bytes 196616 | tf_op jit(solution)/shard_map/ppermute | solution.py:15
  13.1 1.1 copy.88
  14.2 3.6 %collective-permute-start.1 = (bf16[1,32,1,8,128]{4,1,3,2,0:T(8,128)(2,1)S(1)}, bf16[1,32,1,8,128]{4,1,3,2,0:T(8,128)(2,1)S(1)}, u32[]{:S(2)}, u32[]{:S(2)}) collective-permute-start(bf16[1,32,1,8,128]{4,1,3,2,0:T(8,128)(2,1)S(1)} %get-tuple-element.113), channel_id=1, source_target_pairs={{2,0},{4,2},{6,4},{8,6},{10,8},{12,10},{14,12},{0,14},{3,1},{5,3},... | collective-permute-start | bytes 196616 | tf_op jit(solution)/shard_map/ppermute | solution.py:15
  20.6 2.4 collective-permute-done
  23.1 3.4 %collective-permute-start.10 = (bf16[1,32,7,8,1]{4,1,3,2,0:T(8,128)(2,1)S(1)}, bf16[1,32,7,8,1]{4,1,3,2,0:T(8,128)(2,1)S(1)}, u32[]{:S(2)}, u32[]{:S(2)}) collective-permute-start(bf16[1,32,7,8,1]{4,1,3,2,0:T(8,128)(2,1)S(1)} %get-tuple-element.93), channel_id=1, source_target_pairs={{0,1},{1,0},{2,3},{3,2},{4,5},{5,4},{6,7},{7,6},{8,9},{9,8},{10,11... | collective-permute-start | bytes 10760 | tf_op jit(solution)/shard_map/ppermute | solution.py:14
  26.8 3.0 collective-permute-start.2
  29.8 4.7 %collective-permute-done.10 = bf16[1,32,7,8,1]{4,1,3,2,0:T(8,128)(2,1)S(1)} collective-permute-done((bf16[1,32,7,8,1]{4,1,3,2,0:T(8,128)(2,1)S(1)}, bf16[1,32,7,8,1]{4,1,3,2,0:T(8,128)(2,1)S(1)}, u32[]{:S(2)}, u32[]{:S(2)}) %collective-permute-start.10) | collective-permute-done | bytes 3616 | tf_op jit(solution)/shard_map/ppermute | solution.py:14
  34.5 9.8 %collective-permute-done.11 = bf16[1,32,7,8,1]{4,1,3,2,0:T(8,128)(2,1)S(1)} collective-permute-done((bf16[1,32,7,8,1]{4,1,3,2,0:T(8,128)(2,1)S(1)}, bf16[1,32,7,8,1]{4,1,3,2,0:T(8,128)(2,1)S(1)}, u32[]{:S(2)}, u32[]{:S(2)}) %collective-permute-start.11) | collective-permute-done | bytes 3616 | tf_op jit(solution)/shard_map/ppermute | solution.py:15
  44.9 1.5 fusion.148
  46.5 7.7 %collective-permute-done.2 = bf16[1,32,7,8,1]{4,1,3,2,0:T(8,128)(2,1)S(1)} collective-permute-done((bf16[1,32,7,8,1]{4,1,3,2,0:T(8,128)(2,1)S(1)}, bf16[1,32,7,8,1]{4,1,3,2,0:T(8,128)(2,1)S(1)}, u32[]{:S(2)}, u32[]{:S(2)}) %collective-permute-start.2) | collective-permute-done | bytes 3616 | tf_op jit(solution)/shard_map/ppermute | solution.py:14
  54.2 9.8 %collective-permute-done.3 = bf16[1,32,7,8,1]{4,1,3,2,0:T(8,128)(2,1)S(1)} collective-permute-done((bf16[1,32,7,8,1]{4,1,3,2,0:T(8,128)(2,1)S(1)}, bf16[1,32,7,8,1]{4,1,3,2,0:T(8,128)(2,1)S(1)}, u32[]{:S(2)}, u32[]{:S(2)}) %collective-permute-start.3) | collective-permute-done | bytes 3616 | tf_op jit(solution)/shard_map/ppermute | solution.py:15
  64.6 1.5 fusion.150
  67.1 1.1 pad_maximum_fusion.14
  74.3 1.0 convolution_add_fusion.1
  82.5 3.6 %collective-permute-start.5 = (bf16[1,32,1,8,128]{4,1,3,2,0:T(8,128)(2,1)S(1)}, bf16[1,32,1,8,128]{4,1,3,2,0:T(8,128)(2,1)S(1)}, u32[]{:S(2)}, u32[]{:S(2)}) collective-permute-start(bf16[1,32,1,8,128]{4,1,3,2,0:T(8,128)(2,1)S(1)} %get-tuple-element.112), channel_id=1, source_target_pairs={{2,0},{4,2},{6,4},{8,6},{10,8},{12,10},{14,12},{0,14},{3,1},{5,3},... | collective-permute-start | bytes 196616 | tf_op jit(solution)/shard_map/ppermute | solution.py:15
  86.1 1.6 collective-permute-done.4
  88.0 2.8 collective-permute-start.6
  91.0 0.8 maximum_multiply_fusion
  91.8 17.4 %all-reduce.5 = (f32[32]{0:T(128)S(1)}, f32[32]{0:T(128)S(1)}) all-reduce(f32[32]{0:T(128)S(1)} %broadcast_multiply_fusion.1, f32[32]{0:T(128)S(1)} %broadcast_multiply_fusion), channel_id=1, replica_groups=mesh['smp'=8,'gx'=8,'gz'=2] {'smp'}, use_global_device_ids=true, to_apply=%region_3.4 | all-reduce | flops 64 | bytes 512 | tf_op jit(solution)/shard_map/psum | solution.py:104
  109.2 35.0 %all-reduce.3 = (f32[32]{0:T(128)}, f32[32]{0:T(128)}) all-reduce(f32[32]{0:T(128)S(1)} %get-tuple-element.19, f32[32]{0:T(128)S(1)} %get-tuple-element.20), channel_id=1, replica_groups=mesh['smp'=8,'gx'=8,'gz'=2] {'gx','gz'}, use_global_device_ids=true, to_apply=%region_4.5 | all-reduce | flops 64 | bytes 512 | tf_op jit(solution)/shard_map/psum | solution.py:103
  147.1 0.7 convolution_bitcast_fusion.16
  148.4 1.4 fusion.149
  156.3 1.1 convolution_add_fusion.10
  157.5 0.8 maximum_multiply_fusion.1
  158.4 2.2 convolution_add_fusion.9
  160.6 58.4 %all-reduce.12.cloned.1.call-done = (f32[32,3,3,3,32]{4,0,3,2,1:T(8,128)}, f32[32,3,3,3,32]{4,0,3,2,1:T(8,128)}) async-done(((f32[32,3,3,3,32]{4,0,3,2,1:T(8,128)}, f32[32,3,3,3,32]{4,0,3,2,1:T(8,128)}), (f32[32,3,3,3,32]{4,0,3,2,1:T(8,128)}, f32[32,3,3,3,32]{4,0,3,2,1:T(8,128)})) %all-reduce.12.cloned.1.call-update) | async-done | bytes 221200 | tf_op jit(solution)/shard_map/psum | solution.py:104
  219.0 1.4 fusion.12
  220.4 0.9 copy.164
  221.2 87.8 %all-reduce.10.cloned.1.call-done = (f32[32,3,3,3,32]{4,0,3,2,1:T(8,128)}, f32[32,3,3,3,32]{4,0,3,2,1:T(8,128)}) async-done(((f32[32,3,3,3,32]{4,0,3,2,1:T(8,128)}, f32[32,3,3,3,32]{4,0,3,2,1:T(8,128)}), (f32[32,3,3,3,32]{4,0,3,2,1:T(8,128)}, f32[32,3,3,3,32]{4,0,3,2,1:T(8,128)})) %all-reduce.10.cloned.1.call-update) | async-done | bytes 221200 | tf_op jit(solution)/shard_map/psum | solution.py:103
  309.0 1.9 copy.330
  310.9 0.8 copy.331
  (146 shorter events, 29.0 us)
Async XLA Ops:
  7.2 10.6 %copy-start = (bf16[1,32,5,8,128]{4,3,2,1,0:T(8,128)(2,1)S(1)}, bf16[1,32,5,8,128]{4,3,2,1,0:T(8,128)(2,1)}, u32[]{:S(2)}) copy-start(bf16[1,32,5,8,128]{4,3,2,1,0:T(8,128)(2,1)} %param.11) | copy-start | bytes 983044
  7.2 10.9 %copy-start.2 = (bf16[32,3,3,3,32]{4,0,3,2,1:T(8,128)(2,1)S(1)}, bf16[32,3,3,3,32]{4,0,3,2,1:T(8,128)(2,1)}, u32[]{:S(2)}) copy-start(bf16[32,3,3,3,32]{4,0,3,2,1:T(8,128)(2,1)} %param.9) | copy-start | bytes 165892
  7.2 211.8 %all-reduce.12.cloned.1.call-start = ((), (), s32[]{:S(2)}) async-start(), calls=%async_computation.1 | async-start | bytes 1769472 | tf_op jit(solution)/shard_map/psum | solution.py:104
  8.3 12.0 %collective-permute-start.9 = (bf16[1,32,1,8,128]{4,1,3,2,0:T(8,128)(2,1)S(1)}, bf16[1,32,1,8,128]{4,1,3,2,0:T(8,128)(2,1)S(1)}, u32[]{:S(2)}, u32[]{:S(2)}) collective-permute-start(bf16[1,32,1,8,128]{4,1,3,2,0:T(8,128)(2,1)S(1)} %get-tuple-element.109), channel_id=1, source_target_pairs={{2,0},{4,2},{6,4},{8,6},{10,8},{12,10},{14,12},{0,14},{3,1},{5,3},... | collective-permute-start | bytes 196616 | tf_op jit(solution)/shard_map/ppermute | solution.py:15
  13.1 5.1 %copy-start.4 = (bf16[32,3,3,3,32]{4,0,3,2,1:T(8,128)(2,1)S(1)}, bf16[32,3,3,3,32]{4,0,3,2,1:T(8,128)(2,1)}, u32[]{:S(2)}) copy-start(bf16[32,3,3,3,32]{4,0,3,2,1:T(8,128)(2,1)} %param.7) | copy-start | bytes 165892
  13.1 7.2 %collective-permute-start.8 = (bf16[1,32,1,8,128]{4,1,3,2,0:T(8,128)(2,1)S(1)}, bf16[1,32,1,8,128]{4,1,3,2,0:T(8,128)(2,1)S(1)}, u32[]{:S(2)}, u32[]{:S(2)}) collective-permute-start(bf16[1,32,1,8,128]{4,1,3,2,0:T(8,128)(2,1)S(1)} %get-tuple-element.110), channel_id=1, source_target_pairs={{0,2},{2,4},{4,6},{6,8},{8,10},{10,12},{12,14},{14,0},{1,3},{3,5},... | collective-permute-start | bytes 196616 | tf_op jit(solution)/shard_map/ppermute | solution.py:14
  14.2 12.4 %collective-permute-start.1 = (bf16[1,32,1,8,128]{4,1,3,2,0:T(8,128)(2,1)S(1)}, bf16[1,32,1,8,128]{4,1,3,2,0:T(8,128)(2,1)S(1)}, u32[]{:S(2)}, u32[]{:S(2)}) collective-permute-start(bf16[1,32,1,8,128]{4,1,3,2,0:T(8,128)(2,1)S(1)} %get-tuple-element.113), channel_id=1, source_target_pairs={{2,0},{4,2},{6,4},{8,6},{10,8},{12,10},{14,12},{0,14},{3,1},{5,3},... | collective-permute-start | bytes 196616 | tf_op jit(solution)/shard_map/ppermute | solution.py:15
  17.8 5.2 %collective-permute-start = (bf16[1,32,1,8,128]{4,1,3,2,0:T(8,128)(2,1)S(1)}, bf16[1,32,1,8,128]{4,1,3,2,0:T(8,128)(2,1)S(1)}, u32[]{:S(2)}, u32[]{:S(2)}) collective-permute-start(bf16[1,32,1,8,128]{4,1,3,2,0:T(8,128)(2,1)S(1)} %get-tuple-element.114), channel_id=1, source_target_pairs={{0,2},{2,4},{4,6},{6,8},{8,10},{10,12},{12,14},{14,0},{1,3},{3,5},... | collective-permute-start | bytes 196616 | tf_op jit(solution)/shard_map/ppermute | solution.py:14
  20.3 2.7 copy-start.1
  23.1 11.4 %collective-permute-start.10 = (bf16[1,32,7,8,1]{4,1,3,2,0:T(8,128)(2,1)S(1)}, bf16[1,32,7,8,1]{4,1,3,2,0:T(8,128)(2,1)S(1)}, u32[]{:S(2)}, u32[]{:S(2)}) collective-permute-start(bf16[1,32,7,8,1]{4,1,3,2,0:T(8,128)(2,1)S(1)} %get-tuple-element.93), channel_id=1, source_target_pairs={{0,1},{1,0},{2,3},{3,2},{4,5},{5,4},{6,7},{7,6},{8,9},{9,8},{10,11... | collective-permute-start | bytes 10760 | tf_op jit(solution)/shard_map/ppermute | solution.py:14
  26.5 17.9 %collective-permute-start.11 = (bf16[1,32,7,8,1]{4,1,3,2,0:T(8,128)(2,1)S(1)}, bf16[1,32,7,8,1]{4,1,3,2,0:T(8,128)(2,1)S(1)}, u32[]{:S(2)}, u32[]{:S(2)}) collective-permute-start(bf16[1,32,7,8,1]{4,1,3,2,0:T(8,128)(2,1)S(1)} %get-tuple-element.94), channel_id=1, source_target_pairs={{1,0},{0,1},{3,2},{2,3},{5,4},{4,5},{7,6},{6,7},{9,8},{8,9},{11,10... | collective-permute-start | bytes 10760 | tf_op jit(solution)/shard_map/ppermute | solution.py:15
  26.8 27.4 %collective-permute-start.2 = (bf16[1,32,7,8,1]{4,1,3,2,0:T(8,128)(2,1)S(1)}, bf16[1,32,7,8,1]{4,1,3,2,0:T(8,128)(2,1)S(1)}, u32[]{:S(2)}, u32[]{:S(2)}) collective-permute-start(bf16[1,32,7,8,1]{4,1,3,2,0:T(8,128)(2,1)S(1)} %get-tuple-element.101), channel_id=1, source_target_pairs={{0,1},{1,0},{2,3},{3,2},{4,5},{5,4},{6,7},{7,6},{8,9},{9,8},{10,11... | collective-permute-start | bytes 10760 | tf_op jit(solution)/shard_map/ppermute | solution.py:14
  29.8 34.3 %collective-permute-start.3 = (bf16[1,32,7,8,1]{4,1,3,2,0:T(8,128)(2,1)S(1)}, bf16[1,32,7,8,1]{4,1,3,2,0:T(8,128)(2,1)S(1)}, u32[]{:S(2)}, u32[]{:S(2)}) collective-permute-start(bf16[1,32,7,8,1]{4,1,3,2,0:T(8,128)(2,1)S(1)} %get-tuple-element.102), channel_id=1, source_target_pairs={{1,0},{0,1},{3,2},{2,3},{5,4},{4,5},{7,6},{6,7},{9,8},{8,9},{11,10... | collective-permute-start | bytes 10760 | tf_op jit(solution)/shard_map/ppermute | solution.py:15
  70.5 0.7 copy-start.5
  82.4 5.3 %collective-permute-start.4 = (bf16[1,32,1,8,128]{4,1,3,2,0:T(8,128)(2,1)S(1)}, bf16[1,32,1,8,128]{4,1,3,2,0:T(8,128)(2,1)S(1)}, u32[]{:S(2)}, u32[]{:S(2)}) collective-permute-start(bf16[1,32,1,8,128]{4,1,3,2,0:T(8,128)(2,1)S(1)} %get-tuple-element.111), channel_id=1, source_target_pairs={{0,2},{2,4},{4,6},{6,8},{8,10},{10,12},{12,14},{14,0},{1,3},{3,5},... | collective-permute-start | bytes 196616 | tf_op jit(solution)/shard_map/ppermute | solution.py:14
  82.5 5.2 %collective-permute-start.5 = (bf16[1,32,1,8,128]{4,1,3,2,0:T(8,128)(2,1)S(1)}, bf16[1,32,1,8,128]{4,1,3,2,0:T(8,128)(2,1)S(1)}, u32[]{:S(2)}, u32[]{:S(2)}) collective-permute-start(bf16[1,32,1,8,128]{4,1,3,2,0:T(8,128)(2,1)S(1)} %get-tuple-element.112), channel_id=1, source_target_pairs={{2,0},{4,2},{6,4},{8,6},{10,8},{12,10},{14,12},{0,14},{3,1},{5,3},... | collective-permute-start | bytes 196616 | tf_op jit(solution)/shard_map/ppermute | solution.py:15
  88.0 56.3 %collective-permute-start.6 = (bf16[1,32,7,8,1]{4,1,3,2,0:T(8,128)(2,1)S(1)}, bf16[1,32,7,8,1]{4,1,3,2,0:T(8,128)(2,1)S(1)}, u32[]{:S(2)}, u32[]{:S(2)}) collective-permute-start(bf16[1,32,7,8,1]{4,1,3,2,0:T(8,128)(2,1)S(1)} %get-tuple-element.97), channel_id=1, source_target_pairs={{0,1},{1,0},{2,3},{3,2},{4,5},{5,4},{6,7},{7,6},{8,9},{9,8},{10,11... | collective-permute-start | bytes 10760 | tf_op jit(solution)/shard_map/ppermute | solution.py:14
  90.7 53.5 %collective-permute-start.7 = (bf16[1,32,7,8,1]{4,1,3,2,0:T(8,128)(2,1)S(1)}, bf16[1,32,7,8,1]{4,1,3,2,0:T(8,128)(2,1)S(1)}, u32[]{:S(2)}, u32[]{:S(2)}) collective-permute-start(bf16[1,32,7,8,1]{4,1,3,2,0:T(8,128)(2,1)S(1)} %get-tuple-element.98), channel_id=1, source_target_pairs={{1,0},{0,1},{3,2},{2,3},{5,4},{4,5},{7,6},{6,7},{9,8},{8,9},{11,10... | collective-permute-start | bytes 10760 | tf_op jit(solution)/shard_map/ppermute | solution.py:15
  158.4 60.7 %copy-start.6 = (f32[32]{0:T(128)S(1)}, f32[32]{0:T(128)}, u32[]{:S(2)}) copy-start(f32[32]{0:T(128)} %param.10) | copy-start | bytes 388
  158.4 150.6 %all-reduce.10.cloned.1.call-start = ((), (), s32[]{:S(2)}) async-start(), calls=%async_computation | async-start | bytes 1769472 | tf_op jit(solution)/shard_map/psum | solution.py:103
  309.0 1.9 copy-start.3
Sparse Core Ops, SparseCore 0:
  158.5 60.4 all-reduce.11
  222.8 86.1 all-reduce.9
